TPU v7x, 32 devices: a whole 2x2x4 slice. The times are simulated.
32 devices in a mesh: depth: 2 (over core), row: 4 (over y, x), col: 4 (over z).
Axes of the slice: x: 2, y: 2, z: 4, core: 2. Of those that a mesh axis runs over, the one named last changes fastest.
Arguments:
- tile_left: bfloat16 [16, 16, 64, 1024], P('row', 'col'), may hold values from -6 to 6
- tile_right: bfloat16 [16, 16, 64, 1024], P('row', 'col'), may hold values from -6 to 6
- row_left: bfloat16 [16, 8, 64, 1024], P('row', 'depth', None, 'col'), may hold values from -6 to 6
- row_right: bfloat16 [16, 8, 64, 1024], P('row', 'depth', None, 'col'), may hold values from -0.1875 to 0.1875
- col_left: bfloat16 [16, 8, 64, 1024], P('col', 'depth', None, 'row'), may hold values from -6 to 6
- col_right: bfloat16 [16, 8, 64, 1024], P('col', 'depth', None, 'row'), may hold values from -0.1875 to 0.1875
- row_mask: int32 [16, 8], P('row', 'depth'), may hold values 0 or 1
- col_mask: int32 [16, 8], P('col', 'depth'), may hold values 0 or 1
- sketch: bfloat16 [64, 1024], replicated, may hold values from -1 to 1
Outputs:
- new_left: float32 [16, 16, 64, 1024], P('row', 'col', 'depth')
- new_right: float32 [16, 16, 64, 1024], P('row', 'col', 'depth')
All inputs are finite; a program needn't handle non-finite values. No bound on the sum of `row_mask` or of `col_mask` on one device may be relied on, other than what follows from the above.
Results may differ from a plain program's by a relative error of at most 0.0003.
Values may be sent and summed in bfloat16 or wider, within the bound.
No kernel may reach another device: no remote copies, remote signals or barrier semaphores. Data moves between devices by JAX's collectives and lax.ppermute only.
A program may use at most 64 MiB of HBM per device.

v0:
```python
import math
import jax
import jax.numpy as jnp
from jax import lax
from jax.sharding import PartitionSpec as P

NB = 1024
K = 64
exact_mode = lax.Precision.HIGHEST


def orthonormalize(sketched):
    for repeat in range(2):
        gram_mat = jnp.einsum("ijtn,ijsn->ijts", sketched, sketched, precision=exact_mode)
        factor = jnp.linalg.cholesky(gram_mat)
        sketched = jax.scipy.linalg.solve_triangular(factor, sketched, lower=True)
    return sketched


def on_device(
    tile_left, tile_right, row_left, row_right, col_left, col_right, row_mask, col_mask, sketch
):
    row_full_left, row_full_right = (
        lax.all_gather(row_left, "col", axis=3, tiled=True),
        lax.all_gather(row_right, "col", axis=3, tiled=True),
    )
    col_full_left, col_full_right = (
        lax.all_gather(col_left, "row", axis=3, tiled=True),
        lax.all_gather(col_right, "row", axis=3, tiled=True),
    )
    weight_table = (
        row_mask.astype(jnp.float32)[:, None, :] * col_mask.astype(jnp.float32)[None, :, :]
    )
    coupling = jnp.einsum(
        "ikrn,jksn->ijkrs", row_full_right, col_full_right, preferred_element_type=jnp.float32
    )
    coupling = coupling * weight_table[:, :, :, None, None]
    col_sketch = jnp.einsum(
        "jksn,tn->jkst", col_full_left, sketch, preferred_element_type=jnp.float32
    )
    mixing = jnp.einsum("ijkrs,jkst->ijkrt", coupling, col_sketch, precision=exact_mode)
    partial_sketch = -jnp.einsum(
        "ijkrt,ikrn->ijtn",
        mixing,
        row_full_left,
        precision=exact_mode,
        preferred_element_type=jnp.float32,
    )
    sketch_right = jnp.einsum(
        "ijrn,tn->ijrt", tile_right, sketch, preferred_element_type=jnp.float32
    )
    summed = lax.psum(partial_sketch, "depth")
    sketched = summed + jnp.einsum(
        "ijrt,ijrn->ijtn",
        sketch_right,
        tile_left,
        precision=exact_mode,
        preferred_element_type=jnp.float32,
    )
    basis = orthonormalize(sketched)
    rank_rows = K // lax.axis_size("depth")
    rank_offset = lax.axis_index("depth") * rank_rows
    basis_mine = lax.dynamic_slice_in_dim(basis, rank_offset, rank_rows, 2)
    basis_row = jnp.einsum(
        "ijtn,ikrn->ijktr",
        basis,
        row_full_left,
        precision=exact_mode,
        preferred_element_type=jnp.float32,
    )
    projected = jnp.einsum("ijktr,ijkrs->ijkts", basis_row, coupling, precision=exact_mode)
    right_part = -jnp.einsum(
        "ijkts,jksn->ijtn",
        projected,
        col_full_left,
        precision=exact_mode,
        preferred_element_type=jnp.float32,
    )
    right_share = lax.psum_scatter(right_part, "depth", scatter_dimension=2, tiled=True)
    own_part = jnp.einsum(
        "ijtn,ijrn->ijtr",
        basis_mine,
        tile_left,
        precision=exact_mode,
        preferred_element_type=jnp.float32,
    )
    right_share = right_share + jnp.einsum(
        "ijtr,ijrn->ijtn",
        own_part,
        tile_right,
        precision=exact_mode,
        preferred_element_type=jnp.float32,
    )
    return (basis_mine * math.sqrt(NB), right_share / math.sqrt(NB))


def solution(mesh):
    in_specs = (
        P("row", "col", None, None),
        P("row", "col", None, None),
        P("row", "depth", None, "col"),
        P("row", "depth", None, "col"),
        P("col", "depth", None, "row"),
        P("col", "depth", None, "row"),
        P("row", "depth"),
        P("col", "depth"),
        P(),
    )
    out_specs = (P("row", "col", "depth", None), P("row", "col", "depth", None))
    return jax.shard_map(
        on_device, mesh=mesh, in_specs=in_specs, out_specs=out_specs, check_vma=False
    )
```

profile of v0, /device:TPU:0, one launch (start us, length us, event | category | flops | bytes accessed | tf_op | source)
XLA Modules:
  0.0 626.7 jit_solution(12347719536717495241)
XLA Ops:
  7.2 0.0 copy-start
  7.2 0.0 all-gather.5.cloned.1.call-start
  7.3 0.7 all-gather.5.cloned.1.call-update
  8.0 0.0 all-gather.7.cloned.1.call-start
  8.0 1.9 copy.21
  9.9 0.0 all-gather.7.cloned.1.call-update
  9.9 0.0 all-gather.9.cloned.1.call-start
  10.0 0.8 copy.22
  10.8 0.0 all-gather.9.cloned.1.call-update
  10.8 0.0 all-gather.11.cloned.1.call-start
  10.9 0.5 all-gather.11.cloned.1.call-update
  11.4 0.0 all-reduce.2.cloned.1.call-start
  11.5 0.1 copy.23
  11.6 0.1 copy.24
  11.7 0.1 broadcast_multiply_fusion
  11.8 35.9 %all-gather.5.cloned.1.call-done = bf16[4,4,64,1024]{3,2,1,0:T(8,128)(2,1)} async-done(((bf16[4,4,64,256]{3,2,1,0:T(8,128)(2,1)}), bf16[4,4,64,1024]{3,2,1,0:T(8,128)(2,1)}) %all-gather.5.cloned.1.call-update) | async-done | bytes 2097168 | tf_op jit(solution)/shard_map/all_gather | solution.py:28
  47.7 0.0 copy-done.10
  47.7 2.3 convolution_bitcast_fusion
  49.9 35.2 %all-gather.7.cloned.1.call-done = bf16[4,4,64,1024]{3,2,0,1:T(8,128)(2,1)} async-done(((bf16[4,4,64,256]{3,2,0,1:T(8,128)(2,1)}), bf16[4,4,64,1024]{3,2,0,1:T(8,128)(2,1)}) %all-gather.7.cloned.1.call-update) | async-done | bytes 2097168 | tf_op jit(solution)/shard_map/all_gather | solution.py:29
  85.1 48.4 %all-gather.9.cloned.1.call-done = bf16[4,4,64,1024]{3,2,0,1:T(8,128)(2,1)} async-done(((bf16[4,4,64,256]{3,2,0,1:T(8,128)(2,1)}), bf16[4,4,64,1024]{3,2,0,1:T(8,128)(2,1)}) %all-gather.9.cloned.1.call-update) | async-done | bytes 2097168 | tf_op jit(solution)/shard_map/all_gather | solution.py:25
  133.6 3.5 bitcast_multiply_fusion
  137.1 0.0 copy-start.6
  137.1 1.3 copy-done.6
  138.4 3.3 fusion.15
  141.7 37.8 %all-gather.11.cloned.1.call-done = bf16[4,4,64,1024]{3,2,1,0:T(8,128)(2,1)} async-done(((bf16[4,4,64,256]{3,2,1,0:T(8,128)(2,1)}), bf16[4,4,64,1024]{3,2,1,0:T(8,128)(2,1)}) %all-gather.11.cloned.1.call-update) | async-done | bytes 2097168 | tf_op jit(solution)/shard_map/all_gather | solution.py:24
  179.5 6.2 bitcast_negate_fusion.1
  185.6 0.0 all-reduce.2.cloned.1.call-update
  185.6 0.3 reduce-scatter.2.cloned.1.call-start
  186.0 2.7 fusion.32
  188.7 23.4 %all-reduce.2.cloned.1.call-done = f32[4,4,64,1024]{3,2,1,0:T(8,128)} async-done(((f32[4,4,64,1024]{3,2,1,0:T(8,128)}), f32[4,4,64,1024]{3,2,1,0:T(8,128)}) %all-reduce.2.cloned.1.call-update) | async-done | bytes 4194320 | tf_op jit(solution)/shard_map/psum | solution.py:52
  212.1 4.1 convolution_add_fusion
  216.2 1.9 copy-done.2
  218.2 4.0 fusion.36
  222.2 0.2 copy.25
  222.4 0.9 fusion.30
  223.3 95.0 %custom-call.8 = f32[4,4,64,64]{3,2,1,0:T(8,128)S(1)} custom-call(f32[4,4,64,64]{3,2,1,0:T(8,128)} %fusion.30), custom_call_target="Cholesky" | custom-call | tf_op jit(solution)/shard_map/jit(cholesky)/cholesky | solution.py:15
  318.3 0.1 select_reduce_fusion.1
  318.3 0.1 compare_reduce_fusion.1
  318.5 0.1 select_bitcast_fusion.1
  318.6 78.6 %custom-call.9 = f32[4,4,1,64,64]{3,4,2,1,0:T(8,128)S(1)} custom-call(f32[4,4,1,64,64]{4,3,2,1,0:T(8,128)S(1)} %select_bitcast_fusion.1), custom_call_target="InvertDiagBlocksLowerTriangular" | custom-call | tf_op jit(solution)/shard_map/jit(_solve_triangular)/vmap(vmap())/triangular_solve | solution.py:16
  397.3 5.5 fusion.28
  402.8 1.9 copy-done.1
  404.7 4.0 fusion.37
  408.8 0.2 copy.27
  409.0 0.9 fusion.27
  409.8 94.5 %custom-call.10 = f32[4,4,64,64]{3,2,1,0:T(8,128)S(1)} custom-call(f32[4,4,64,64]{3,2,1,0:T(8,128)} %fusion.27), custom_call_target="Cholesky" | custom-call | tf_op jit(solution)/shard_map/jit(cholesky)/cholesky | solution.py:15
  504.3 0.1 select_reduce_fusion
  504.4 0.1 compare_reduce_fusion
  504.6 0.1 select_bitcast_fusion
  504.7 78.6 %custom-call.11 = f32[4,4,1,64,64]{3,4,2,1,0:T(8,128)S(1)} custom-call(f32[4,4,1,64,64]{4,3,2,1,0:T(8,128)S(1)} %select_bitcast_fusion), custom_call_target="InvertDiagBlocksLowerTriangular" | custom-call | tf_op jit(solution)/shard_map/jit(_solve_triangular)/vmap(vmap())/triangular_solve | solution.py:16
  583.3 0.0 copy-start.5
  583.4 5.8 fusion.25
  589.2 3.5 fusion
  592.6 0.0 copy-start.7
  592.7 1.4 copy.61
  594.1 0.2 copy-done.7
  594.2 3.5 fusion.12
  597.8 3.7 fusion.2
  601.4 0.0 reduce-scatter.2.cloned.1.call-update
  601.5 3.4 dynamic-slice_multiply_fusion
  604.9 1.8 fusion.17
  606.7 8.1 %reduce-scatter.2.cloned.1.call-done = f32[4,4,32,1024]{3,2,0,1:T(8,128)} async-done(((f32[4,4,64,1024]{3,2,0,1:T(8,128)}), f32[4,4,32,1024]{3,2,0,1:T(8,128)}) %reduce-scatter.2.cloned.1.call-update) | async-done | bytes 2097168 | tf_op jit(solution)/shard_map/reduce_scatter | solution.py:79
  614.8 3.3 add_multiply_fusion
  618.2 1.5 copy.30
  (21 shorter events, 0.1 us)
Async XLA Ops:
  7.2 204.9 %copy-start = (bf16[4,4,64,1024]{3,2,1,0:T(8,128)(2,1)S(1)}, bf16[4,4,64,1024]{3,2,1,0:T(8,128)(2,1)}, u32[]{:S(2)}) copy-start(bf16[4,4,64,1024]{3,2,1,0:T(8,128)(2,1)} %param.12) | copy-start | bytes 6291460
  7.2 2.8 copy-start.9
  7.2 4.3 copy-start.11
  7.2 4.4 copy-start.12
  7.2 40.4 %copy-start.10 = (bf16[64,1024]{1,0:T(8,128)(2,1)S(1)}, bf16[64,1024]{1,0:T(8,128)(2,1)}, u32[]{:S(2)}) copy-start(bf16[64,1024]{1,0:T(8,128)(2,1)} %param.20) | copy-start | bytes 393220
  7.2 40.4 %all-gather.5.cloned.1.call-start = ((), (), s32[]{:S(2)}) async-start(), calls=%async_computation.1 | async-start | bytes 2621440 | tf_op jit(solution)/shard_map/all_gather | solution.py:28
  8.0 77.2 %all-gather.7.cloned.1.call-start = ((), (), s32[]{:S(2)}) async-start(), calls=%async_computation.2 | async-start | bytes 2621440 | tf_op jit(solution)/shard_map/all_gather | solution.py:29
  9.9 123.6 %all-gather.9.cloned.1.call-start = ((), (), s32[]{:S(2)}) async-start(), calls=%async_computation.3 | async-start | bytes 2621440 | tf_op jit(solution)/shard_map/all_gather | solution.py:25
  10.8 168.6 %all-gather.11.cloned.1.call-start = ((), (), s32[]{:S(2)}) async-start(), calls=%async_computation.4 | async-start | bytes 2621440 | tf_op jit(solution)/shard_map/all_gather | solution.py:24
  11.4 200.7 %all-reduce.2.cloned.1.call-start = ((), (), s32[]{:S(2)}) async-start(), calls=%async_computation.5 | async-start | bytes 8388608 | tf_op jit(solution)/shard_map/psum | solution.py:52
  137.1 1.3 copy-start.6
  185.6 429.2 %reduce-scatter.2.cloned.1.call-start = ((), (), s32[]{:S(2)}) async-start(), calls=%async_computation.6 | async-start | bytes 6291456 | tf_op jit(solution)/shard_map/reduce_scatter | solution.py:79
  216.2 1.9 copy-start.2
  402.8 1.9 copy-start.1
  583.3 5.8 copy-start.5
  589.2 3.5 copy-start.3
  592.6 1.6 copy-start.7
  594.2 3.5 copy-start.8
  601.5 3.4 copy-start.4
Sparse Core Ops, SparseCore 0:
  9.9 37.7 all-gather.4
  50.1 35.0 all-gather.6
  87.3 46.2 all-gather.8
  135.0 44.4 all-gather.10
  185.8 26.2 all-reduce.1
  601.6 13.2 reduce-scatter.1
where the time goes:
time: 632 us; the launch traced here: 627 us
  other arithmetic  353 us (56%)
  waiting for transfers between devices  190 us (30%)
  matrix products  57.2 us (9%)
  between operations  14.6 us (2%)
  local copies, waits for them, and re-layouts  11.6 us (2%)
    another operation x7, other arithmetic, orthonormalize(): factor = jnp.linalg.cholesky(gram_mat)  190 us
    another operation x5, other arithmetic, orthonormalize(): sketched = jax.scipy.linalg.solve_triangular(factor, sketched, lower=True)  158 us
    all_gather x1, waiting for transfers between devices, on_device(): lax.all_gather(row_right, 'col', axis=3, tiled=True)  48.4 us
    all_gather x1, waiting for transfers between devices, on_device(): lax.all_gather(row_left, 'col', axis=3, tiled=True)  37.8 us
    all_gather x1, waiting for transfers between devices, on_device(): lax.all_gather(col_left, 'row', axis=3, tiled=True)  35.9 us
    all_gather x1, waiting for transfers between devices, on_device(): lax.all_gather(col_right, 'row', axis=3, tiled=True)  35.2 us
    psum x1, waiting for transfers between devices, on_device(): summed = lax.psum(partial_sketch, 'depth')  23.4 us
  transfers between devices with their start and end apart: 6, of which 6 were waited for; matrix products, arithmetic and copies ran while one was open for 3% of the time, Pallas kernels for 0%

commit v1 on v0

--- a/solution.py
+++ b/solution.py
@@ -24,8 +24,11 @@
         lax.all_gather(row_left, "col", axis=3, tiled=True),
         lax.all_gather(row_right, "col", axis=3, tiled=True),
     )
+    play_the_slices = lambda values: jnp.concatenate(
+        lax.all_to_all(jnp.stack([values] * lax.axis_size("row")), "row", 0, 0), axis=3
+    )
     col_full_left, col_full_right = (
-        lax.all_gather(col_left, "row", axis=3, tiled=True),
+        play_the_slices(col_left),
         lax.all_gather(col_right, "row", axis=3, tiled=True),
     )
     weight_table = (

time: 632 us -> 610 us (0.965)
  waiting for transfers between devices: 190 us -> 150 us
  local copies, waits for them, and re-layouts: 11.6 us -> 24.7 us
    all_gather x1 -> x0, waiting for transfers between devices: 35.9 us -> none  [on_device(): lax.all_gather(col_left, 'row', axis=3, tiled=True)]
    all_to_all x0 -> x1, waiting for transfers between devices: none -> 31 us  [on_device(): lax.all_to_all(jnp.stack([values] * lax.axis_size('row')), 'row', 0, 0)]
    all_gather x1, waiting for transfers between devices: 35.2 us -> 10.3 us  [on_device(): lax.all_gather(col_right, 'row', axis=3, tiled=True)]
    reshape x0 -> x3, local copies, waits for them, and re-layouts: none -> 11.9 us  [on_device(): jnp.concatenate(lax.all_to_all(jnp.stack([values] * lax.axis_size('row'))...]
    psum x1, waiting for transfers between devices: 23.4 us -> 13.7 us  [on_device(): summed = lax.psum(partial_sketch, 'depth')]
  transfers between devices with their start and end apart: 6 -> 6, of which waited for: 6 -> 6; matrix products, arithmetic and copies ran while one was open for 3% -> 5% of each run, Pallas kernels for 0% -> 0%
where the time goes in v1:
time: 610 us; the launch traced here: 603 us
  other arithmetic  352 us (58%)
  waiting for transfers between devices  150 us (25%)
  matrix products  55.8 us (9%)
  local copies, waits for them, and re-layouts  24.7 us (4%)
  between operations  14.3 us (2%)
    another operation x7, other arithmetic, orthonormalize(): factor = jnp.linalg.cholesky(gram_mat)  189 us
    another operation x5, other arithmetic, orthonormalize(): sketched = jax.scipy.linalg.solve_triangular(factor, sketched, lower=True)  158 us
    all_gather x1, waiting for transfers between devices, on_device(): lax.all_gather(row_right, 'col', axis=3, tiled=True)  48.4 us
    all_gather x1, waiting for transfers between devices, on_device(): lax.all_gather(row_left, 'col', axis=3, tiled=True)  38.1 us
    all_to_all x1, waiting for transfers between devices, on_device(): lax.all_to_all(jnp.stack([values] * lax.axis_size('row')), 'row', 0, 0)  31 us
    psum x1, waiting for transfers between devices, on_device(): summed = lax.psum(partial_sketch, 'depth')  13.7 us
  transfers between devices with their start and end apart: 6, of which 6 were waited for; matrix products, arithmetic and copies ran while one was open for 5% of the time, Pallas kernels for 0%

profile of v1, /device:TPU:0, one launch (start us, length us, event | category | flops | bytes accessed | tf_op | source)
XLA Modules:
  0.0 603.0 jit_solution(915645128005304492)
XLA Ops:
  7.2 0.0 copy-start
  7.2 0.0 all-gather.4.cloned.1.call-start
  7.2 2.1 copy.33
  9.3 0.0 all-gather.4.cloned.1.call-update
  9.3 0.0 all-gather.6.cloned.1.call-start
  9.4 1.9 copy.34
  11.3 0.0 all-gather.6.cloned.1.call-update
  11.3 0.0 all-gather.8.cloned.1.call-start
  11.3 0.7 all-gather.8.cloned.1.call-update
  12.0 0.0 copy-done.9
  12.0 1.6 stack.2
  13.6 5.3 all-to-all-start
  19.0 0.1 copy.35
  19.1 0.1 copy.36
  19.2 0.1 broadcast_multiply_fusion
  19.2 31.0 %all-to-all-done = bf16[4,4,4,64,256]{4,3,2,1,0:T(8,128)(2,1)} async-done(((bf16[4,4,4,64,256]{4,3,2,1,0:T(8,128)(2,1)}), bf16[4,4,4,64,256]{4,3,2,1,0:T(8,128)(2,1)}, u32[]{:S(2)}, u32[]{:S(2)}) %all-to-all-start) | async-done | bytes 2097184 | tf_op jit(solution)/shard_map/all_to_all | solution.py:28
  50.3 2.0 copy.67
  52.3 1.1 convolution_bitcast_fusion
  53.4 10.3 %all-gather.4.cloned.1.call-done = bf16[4,4,64,1024]{3,2,0,1:T(8,128)(2,1)} async-done(((bf16[4,4,64,256]{3,2,0,1:T(8,128)(2,1)}), bf16[4,4,64,1024]{3,2,0,1:T(8,128)(2,1)}) %all-gather.4.cloned.1.call-update) | async-done | bytes 2097168 | tf_op jit(solution)/shard_map/all_gather | solution.py:32
  63.7 48.4 %all-gather.6.cloned.1.call-done = bf16[4,4,64,1024]{3,2,0,1:T(8,128)(2,1)} async-done(((bf16[4,4,64,256]{3,2,0,1:T(8,128)(2,1)}), bf16[4,4,64,1024]{3,2,0,1:T(8,128)(2,1)}) %all-gather.6.cloned.1.call-update) | async-done | bytes 2097168 | tf_op jit(solution)/shard_map/all_gather | solution.py:25
  112.1 3.5 bitcast_multiply_fusion
  115.6 0.0 copy-start.6
  115.6 1.3 copy-done.6
  116.9 3.1 fusion.12
  120.1 38.1 %all-gather.8.cloned.1.call-done = bf16[4,4,64,1024]{3,2,1,0:T(8,128)(2,1)} async-done(((bf16[4,4,64,256]{3,2,1,0:T(8,128)(2,1)}), bf16[4,4,64,1024]{3,2,1,0:T(8,128)(2,1)}) %all-gather.8.cloned.1.call-update) | async-done | bytes 2097168 | tf_op jit(solution)/shard_map/all_gather | solution.py:24
  158.2 6.2 %bitcast_negate_fusion.1 = f32[4,4,64,1024]{3,2,1,0:T(8,128)} fusion(bf16[4,4,64,1024]{3,2,1,0:T(8,128)(2,1)} %all-gather.8.cloned.1.call-done, f32[4,4,64,4,64]{4,2,1,0,3:T(8,128)} %fusion.12), kind=kOutput, calls=%fused_computation.4 | convolution fusion | flops 3222274048 | bytes 7340032 | tf_op jit(solution)/shard_map/ijkrt,ikrn->ijtn/dot_general | solution.py:45
  164.3 0.0 all-reduce.2.cloned.1.call-update
  164.4 0.0 reduce-scatter.2.cloned.1.call-start
  164.4 2.7 fusion.37
  167.1 5.0 copy.32
  172.1 4.9 reshape.33
  177.1 13.7 %all-reduce.2.cloned.1.call-done = f32[4,4,64,1024]{3,2,1,0:T(8,128)} async-done(((f32[4,4,64,1024]{3,2,1,0:T(8,128)}), f32[4,4,64,1024]{3,2,1,0:T(8,128)}) %all-reduce.2.cloned.1.call-update) | async-done | bytes 4194320 | tf_op jit(solution)/shard_map/psum | solution.py:55
  190.8 4.1 convolution_add_fusion
  194.9 1.9 copy-done.2
  196.9 4.0 fusion.41
  200.9 0.2 copy.40
  201.1 0.9 fusion.35
  202.0 94.5 %custom-call.8 = f32[4,4,64,64]{3,2,1,0:T(8,128)S(1)} custom-call(f32[4,4,64,64]{3,2,1,0:T(8,128)} %fusion.35), custom_call_target="Cholesky" | custom-call | tf_op jit(solution)/shard_map/jit(cholesky)/cholesky | solution.py:15
  296.5 0.1 select_reduce_fusion.1
  296.5 0.1 compare_reduce_fusion.1
  296.7 0.1 select_bitcast_fusion.1
  296.8 78.6 %custom-call.9 = f32[4,4,1,64,64]{3,4,2,1,0:T(8,128)S(1)} custom-call(f32[4,4,1,64,64]{4,3,2,1,0:T(8,128)S(1)} %select_bitcast_fusion.1), custom_call_target="InvertDiagBlocksLowerTriangular" | custom-call | tf_op jit(solution)/shard_map/jit(_solve_triangular)/vmap(vmap())/triangular_solve | solution.py:16
  375.5 5.7 fusion.33
  381.2 1.9 copy-done.1
  383.1 4.0 fusion.42
  387.1 0.2 copy.42
  387.4 0.9 fusion.32
  388.2 94.5 %custom-call.10 = f32[4,4,64,64]{3,2,1,0:T(8,128)S(1)} custom-call(f32[4,4,64,64]{3,2,1,0:T(8,128)} %fusion.32), custom_call_target="Cholesky" | custom-call | tf_op jit(solution)/shard_map/jit(cholesky)/cholesky | solution.py:15
  482.7 0.1 select_reduce_fusion
  482.8 0.1 compare_reduce_fusion
  482.9 0.1 select_bitcast_fusion
  483.1 78.6 %custom-call.11 = f32[4,4,1,64,64]{3,4,2,1,0:T(8,128)S(1)} custom-call(f32[4,4,1,64,64]{4,3,2,1,0:T(8,128)S(1)} %select_bitcast_fusion), custom_call_target="InvertDiagBlocksLowerTriangular" | custom-call | tf_op jit(solution)/shard_map/jit(_solve_triangular)/vmap(vmap())/triangular_solve | solution.py:16
  561.7 0.0 copy-start.5
  561.7 5.8 fusion.30
  567.6 0.0 copy-start.7
  567.6 3.5 fusion.23
  571.1 3.5 fusion.7
  574.6 3.5 fusion.2
  578.1 0.0 reduce-scatter.2.cloned.1.call-update
  578.1 3.4 dynamic-slice_multiply_fusion
  581.5 1.8 fusion.17
  583.3 8.1 %reduce-scatter.2.cloned.1.call-done = f32[4,4,32,1024]{3,2,0,1:T(8,128)} async-done(((f32[4,4,64,1024]{3,2,0,1:T(8,128)}), f32[4,4,32,1024]{3,2,0,1:T(8,128)}) %reduce-scatter.2.cloned.1.call-update) | async-done | bytes 2097168 | tf_op jit(solution)/shard_map/reduce_scatter | solution.py:82
  591.5 3.3 add_multiply_fusion
  594.8 1.5 copy.47
  (23 shorter events, 0.1 us)
Async XLA Ops:
  7.2 183.6 %copy-start = (bf16[4,4,64,1024]{3,2,1,0:T(8,128)(2,1)S(1)}, bf16[4,4,64,1024]{3,2,1,0:T(8,128)(2,1)}, u32[]{:S(2)}) copy-start(bf16[4,4,64,1024]{3,2,1,0:T(8,128)(2,1)} %param.12) | copy-start | bytes 6291460
  7.2 4.8 copy-start.9
  7.2 56.5 %all-gather.4.cloned.1.call-start = ((), (), s32[]{:S(2)}) async-start(), calls=%async_computation.2 | async-start | bytes 2621440 | tf_op jit(solution)/shard_map/all_gather | solution.py:32
  9.3 102.8 %all-gather.6.cloned.1.call-start = ((), (), s32[]{:S(2)}) async-start(), calls=%async_computation.3 | async-start | bytes 2621440 | tf_op jit(solution)/shard_map/all_gather | solution.py:25
  11.3 146.9 %all-gather.8.cloned.1.call-start = ((), (), s32[]{:S(2)}) async-start(), calls=%async_computation.4 | async-start | bytes 2621440 | tf_op jit(solution)/shard_map/all_gather | solution.py:24
  13.6 5.3 copy-start.11
  13.6 5.4 copy-start.12
  13.6 36.6 %all-to-all-start = ((bf16[4,4,4,64,256]{4,3,2,1,0:T(8,128)(2,1)}), bf16[4,4,4,64,256]{4,3,2,1,0:T(8,128)(2,1)}, u32[]{:S(2)}, u32[]{:S(2)}) async-start(bf16[4,4,4,64,256]{4,3,2,1,0:T(8,128)(2,1)} %stack.2), calls=%async_computation | async-start | bytes 4194304 | tf_op jit(solution)/shard_map/all_to_all | solution.py:28
  19.0 171.8 %all-reduce.2.cloned.1.call-start = ((), (), s32[]{:S(2)}) async-start(), calls=%async_computation.5 | async-start | bytes 8388608 | tf_op jit(solution)/shard_map/psum | solution.py:55
  50.3 2.0 copy-start.10
  115.6 1.3 copy-start.6
  164.4 427.1 %reduce-scatter.2.cloned.1.call-start = ((), (), s32[]{:S(2)}) async-start(), calls=%async_computation.6 | async-start | bytes 6291456 | tf_op jit(solution)/shard_map/reduce_scatter | solution.py:82
  194.9 2.0 copy-start.2
  381.2 2.0 copy-start.1
  561.7 5.9 copy-start.5
  567.6 3.5 copy-start.3
  567.6 3.5 copy-start.7
  571.1 3.5 copy-start.8
  578.1 3.4 copy-start.4
Sparse Core Ops, SparseCore 0:
  9.8 53.8 all-gather.3
  65.8 46.2 all-gather.5
  113.7 44.4 all-gather.7
  164.5 26.2 all-reduce.1
  578.2 13.2 reduce-scatter.1
